TPU v7x, 512 devices: a whole 4x8x8 slice. The times are simulated.
512 devices in a mesh: tm: 32 (over y, z_lo, core), chan: 16 (over z_hi, x).
Axes of the slice: x: 4, y: 8, z: 8 (z_hi: 4, z_lo: 2; z = z_hi * 2 + z_lo), core: 2. Of those that a mesh axis runs over, the one named last changes fastest.
Arguments:
- record: bfloat16 [2048, 49152], P('chan', 'tm'), may hold values from -250 to 250
- offsets: int32 [4], replicated, may hold values from 0 to 37152, as said below
- dead_mask: int32 [2048], P('chan'), may hold values 0 or 1
- sources: int32 [128], replicated, may hold values from 0 to 2047
Outputs:
- cross_spectra: float32 [640, 2, 128, 2048], P('tm', None, None, 'chan')
Inputs may be any that keep to these rules, and one draw needn't show every extreme that they name: offsets[w] lies between w * 12000 and w * 12000 + 49152 - 4 * 12000; offsets[0] is 0 and the last window ends at the record's last sample.
All inputs are finite; a program needn't handle non-finite values. No bound on the sum of `dead_mask` on one device may be relied on, other than what follows from the above.
Results may differ from a plain program's by a relative error of at most 0.002.
The roundings to bfloat16 on the way count: a program that leaves them out, or rounds other values in their place, can miss the bound.
Values may be sent and summed in bfloat16 or wider, within the bound.
A program may use at most 128 MiB of HBM per device.

v0:
```python
import math
import jax
import jax.numpy as jnp
from jax import lax
from jax.sharding import PartitionSpec as P

W = 12000
F = 640
FLO = 6
NWIN = 4


def band_basis(first_bin, width, times):
    bins = first_bin + jnp.arange(width, dtype=jnp.int32)
    phase = times[:, None] * bins[None, :] % W
    angle = phase.astype(jnp.float32) * (2.0 * math.pi / W)
    return jnp.stack([jnp.cos(angle), -jnp.sin(angle)], axis=-1)


def amplitude(fourier_coefficients):
    return jnp.sqrt(fourier_coefficients[:, :, 0] ** 2 + fourier_coefficients[:, :, 1] ** 2)


def whiten(fourier_coefficients, magnitude, level):
    denominator = magnitude + 0.1 * level[None] + 1e-06
    return (fourier_coefficients / denominator[:, :, None, :]).astype(jnp.bfloat16)


def shards(record, offsets, dead_mask, sources):
    tm_count = lax.axis_size("tm")
    bins_dev = F // tm_count
    channels = record.shape[0]
    group_first = lax.axis_index("tm") * record.shape[1]
    local_times = group_first + jnp.arange(record.shape[1], dtype=jnp.int32)
    start = jnp.int32(0)
    blocks = []
    for first in range(0, lax.axis_size("tm") * bins_dev, 64):
        width = min(64, lax.axis_size("tm") * bins_dev - first)
        per_window = []
        for window in range(NWIN):
            shifted = local_times - offsets[window]
            inside = (shifted >= 0) & (shifted < W)
            basis = band_basis(FLO + start + first, width, jnp.where(inside, shifted, 0))
            basis = (basis * inside[:, None, None].astype(jnp.float32)).astype(jnp.bfloat16)
            per_window.append(
                jnp.einsum("ct,tfp->fpc", record, basis, preferred_element_type=jnp.float32)
            )
        blocks.append(jnp.stack(per_window, axis=1))
    fourier_coefficients = lax.psum_scatter(
        jnp.concatenate(blocks, axis=0), "tm", scatter_dimension=0, tiled=True
    )
    magnitude = amplitude(fourier_coefficients)
    level = lax.psum(jnp.sum(magnitude, axis=0), "tm") / F
    white = whiten(fourier_coefficients, magnitude, level)
    white = white * dead_mask.astype(jnp.bfloat16)[None, None, None, :]
    local_index = sources - lax.axis_index("chan") * channels
    onehot = (jnp.arange(channels, dtype=jnp.int32)[:, None] == local_index[None, :]).astype(
        jnp.bfloat16
    )
    selected_bins = jnp.einsum("fwpc,cs->fwps", white, onehot, preferred_element_type=jnp.float32)
    source_spec = lax.psum(selected_bins.astype(jnp.bfloat16), "chan")
    left_channel = source_spec.reshape(bins_dev, NWIN * 2, source_spec.shape[3])
    right_channel_real = white.reshape(bins_dev, NWIN * 2, channels)
    right_channel_imaginary = jnp.concatenate(
        [white[:, :, 1:2], -white[:, :, 0:1]], axis=2
    ).reshape(bins_dev, NWIN * 2, channels)
    real_component = jnp.einsum(
        "qia,qie->qae", left_channel, right_channel_real, preferred_element_type=jnp.float32
    )
    imaginary_component = jnp.einsum(
        "qia,qie->qae", left_channel, right_channel_imaginary, preferred_element_type=jnp.float32
    )
    return jnp.stack([real_component, imaginary_component], axis=1) / NWIN


def solution(mesh):
    return jax.shard_map(
        shards,
        mesh=mesh,
        in_specs=(P("chan", "tm"), P(), P("chan"), P()),
        out_specs=P("tm", None, None, "chan"),
        check_vma=False,
    )
```

profile of v0, /device:TPU:32, one launch (start us, length us, event | category | flops | bytes accessed | tf_op | source)
XLA Modules:
  0.0 483.6 jit_solution(6104584640488371410)
XLA Ops:
  6.6 1.5 fusion.474
  8.1 1.3 fusion.412
  9.4 1.3 fusion.428
  10.7 1.2 fusion.418
  12.0 1.2 fusion.430
  13.3 64.1 %fusion.202 = (f32[1536,64,1]{0,1,2:T(8,128)S(1)}, f32[1536,64,1]{0,1,2:T(8,128)S(1)}, f32[1536,64,1]{0,1,2:T(8,128)S(1)}, f32[1536,64,1]{0,1,2:T(8,128)S(1)}, f...) fusion(s32[64]{0:T(128)S(1)} %get-tuple-element.231, ...), kind=kLoop, calls=%fused_computation.288 | loop fusion | flops 39321600 | bytes 31484416 | tf_op jit(solution)/shard_map/cos | solution.py:17
  77.4 0.3 convolution_bitcast_fusion.5
  77.7 0.3 convolution_bitcast_fusion.9
  77.9 0.3 convolution_bitcast_fusion.4
  78.2 0.3 convolution_bitcast_fusion.8
  78.5 0.3 convolution_bitcast_fusion.3
  88.5 3.2 copy.14
  91.7 0.6 copy-done.1
  92.3 1.3 dynamic-slice
  94.4 238.8 %all-reduce.3.cloned.1.call-done = f32[640,4,2,128]{3,1,2,0:T(4,128)} async-done(((f32[640,4,2,128]{3,1,2,0:T(4,128)}), f32[640,4,2,128]{3,1,2,0:T(4,128)}) %all-reduce.3.cloned.1.call-update) | async-done | bytes 2621456
  333.2 0.8 fusion.472
  334.0 55.1 %psum.14 = f32[4,128]{1,0:T(4,128)S(1)} all-reduce(f32[4,128]{1,0:T(4,128)S(1)} %fusion.472), channel_id=1, replica_groups=mesh['tm'=32,'chan'=16] {'tm'}, use_global_device_ids=true, to_apply=%region_2.3 | all-reduce | flops 512 | bytes 4096 | tf_op jit(solution)/shard_map/psum | solution.py:53
  389.2 0.8 add_bitcast_fusion
  390.0 0.9 fusion.406
  391.2 82.7 %psum.15 = bf16[20,8,128]{2,1,0:T(8,128)(2,1)S(1)} all-reduce(bf16[20,8,128]{2,1,0:T(8,128)(2,1)S(1)} %copy.16), channel_id=1, replica_groups=mesh['tm'=32,'chan'=16] {'chan'}, use_global_device_ids=true, to_apply=%region_3.4 | all-reduce | flops 20480 | bytes 81920 | tf_op jit(solution)/shard_map/psum | solution.py:61
  473.9 0.4 convolution_bitcast_fusion.1
  474.3 0.4 convolution_bitcast_fusion
  474.7 0.3 maximum_multiply_fusion
  475.0 1.7 copy.19
  (66 shorter events, 9.8 us)
Async XLA Ops:
  6.5 70.8 %copy-start = (bf16[128,1536]{1,0:T(8,128)(2,1)S(1)}, bf16[128,1536]{1,0:T(8,128)(2,1)}, u32[]{:S(2)}) copy-start(bf16[128,1536]{1,0:T(8,128)(2,1)} %param.4) | copy-start | bytes 1179652
  6.5 326.7 %all-reduce.3.cloned.1.call-start = ((), (), s32[]{:S(2)}) async-start(), calls=%async_computation | async-start | bytes 5242880
  91.7 0.7 copy-start.1
  91.7 2.7 copy-start.2
Sparse Core Ops, SparseCore 0:
  91.8 241.3 all-reduce.2
where the time goes:
time: 484 us
  waiting for transfers between devices  239 us (49%)
  blocking collectives  138 us (29%)
  other arithmetic  72.5 us (15%)
  between operations  14.6 us (3%)
  matrix products  11.5 us (2%)
  local copies, waits for them, and re-layouts  8.37 us (2%)
    unnamed x2, waiting for transfers between devices  239 us
    psum x1, blocking collectives, shards(): source_spec = lax.psum(selected_bins.astype(jnp.bfloat16), 'chan')  82.7 us
    cos x1, other arithmetic, band_basis(): return jnp.stack([jnp.cos(angle), -jnp.sin(angle)], axis=-1)  64.1 us
    psum x1, blocking collectives, shards(): level = lax.psum(jnp.sum(magnitude, axis=0), 'tm') / F  55.1 us
    dot_general x40, matrix products, shards(): jnp.einsum('ct,tfp->fpc', record, basis, preferred_element_type=jnp.float32)  10.5 us
  transfers between devices with their start and end apart: 1, of which 1 were waited for; matrix products, arithmetic and copies ran while one was open for 0% of the time, Pallas kernels for 0%

commit v1 on v0

--- a/solution.py
+++ b/solution.py
@@ -50,7 +50,7 @@
         jnp.concatenate(blocks, axis=0), "tm", scatter_dimension=0, tiled=True
     )
     magnitude = amplitude(fourier_coefficients)
-    level = lax.psum(jnp.sum(magnitude, axis=0), "tm") / F
+    level = jnp.sum(lax.all_gather(jnp.sum(magnitude, axis=0), "tm"), axis=0) / F
     white = whiten(fourier_coefficients, magnitude, level)
     white = white * dead_mask.astype(jnp.bfloat16)[None, None, None, :]
     local_index = sources - lax.axis_index("chan") * channels

time: 484 us -> 461 us (0.952)
  blocking collectives: 138 us -> 115 us
    psum x1 -> x0, blocking collectives: 55.1 us -> none  [shards(): level = lax.psum(jnp.sum(magnitude, axis=0), 'tm') / F]
    all_gather x0 -> x1, blocking collectives: none -> 31 us  [shards(): lax.all_gather(jnp.sum(magnitude, axis=0), 'tm')]
where the time goes in v1:
time: 461 us
  waiting for transfers between devices  239 us (52%)
  blocking collectives  115 us (25%)
  other arithmetic  72.5 us (16%)
  between operations  14.6 us (3%)
  matrix products  11.5 us (2%)
  local copies, waits for them, and re-layouts  8.37 us (2%)
    unnamed x2, waiting for transfers between devices  239 us
    psum x1, blocking collectives, shards(): source_spec = lax.psum(selected_bins.astype(jnp.bfloat16), 'chan')  84 us
    cos x1, other arithmetic, band_basis(): return jnp.stack([jnp.cos(angle), -jnp.sin(angle)], axis=-1)  64.1 us
    all_gather x1, blocking collectives, shards(): lax.all_gather(jnp.sum(magnitude, axis=0), 'tm')  31 us
    dot_general x40, matrix products, shards(): jnp.einsum('ct,tfp->fpc', record, basis, preferred_element_type=jnp.float32)  10.5 us
  transfers between devices with their start and end apart: 1, of which 1 were waited for; matrix products, arithmetic and copies ran while one was open for 0% of the time, Pallas kernels for 0%

profile of v1, /device:TPU:32, one launch (start us, length us, event | category | flops | bytes accessed | tf_op | source)
XLA Modules:
  0.0 460.8 jit_solution(4089145924357329478)
XLA Ops:
  6.6 1.5 fusion.474
  8.1 1.3 fusion.412
  9.4 1.3 fusion.428
  10.7 1.2 fusion.418
  12.0 1.2 fusion.430
  13.3 64.1 %fusion.202 = (f32[1536,64,1]{0,1,2:T(8,128)S(1)}, f32[1536,64,1]{0,1,2:T(8,128)S(1)}, f32[1536,64,1]{0,1,2:T(8,128)S(1)}, f32[1536,64,1]{0,1,2:T(8,128)S(1)}, f...) fusion(s32[64]{0:T(128)S(1)} %get-tuple-element.231, ...), kind=kLoop, calls=%fused_computation.288 | loop fusion | flops 39321600 | bytes 31484416 | tf_op jit(solution)/shard_map/cos | solution.py:17
  77.4 0.3 convolution_bitcast_fusion.5
  77.7 0.3 convolution_bitcast_fusion.9
  77.9 0.3 convolution_bitcast_fusion.4
  78.2 0.3 convolution_bitcast_fusion.8
  78.5 0.3 convolution_bitcast_fusion.3
  88.5 3.2 copy.14
  91.7 0.6 copy-done.1
  92.3 1.3 dynamic-slice
  94.4 238.8 %all-reduce.3.cloned.1.call-done = f32[640,4,2,128]{3,1,2,0:T(4,128)} async-done(((f32[640,4,2,128]{3,1,2,0:T(4,128)}), f32[640,4,2,128]{3,1,2,0:T(4,128)}) %all-reduce.3.cloned.1.call-update) | async-done | bytes 2621456
  333.2 0.8 fusion.472
  334.0 31.0 %all-gather.1 = f32[32,4,128]{2,1,0:T(4,128)S(1)} all-gather(f32[1,4,128]{2,1,0:T(4,128)S(1)} %bitcast.188), channel_id=2, replica_groups=mesh['tm'=32,'chan'=16] {'tm'}, dimensions={0}, use_global_device_ids=true | all-gather | bytes 67584 | tf_op jit(solution)/shard_map/all_gather | solution.py:53
  365.1 0.8 add_bitcast_fusion
  365.9 0.9 fusion.406
  367.1 84.0 %psum.7 = bf16[20,8,128]{2,1,0:T(8,128)(2,1)S(1)} all-reduce(bf16[20,8,128]{2,1,0:T(8,128)(2,1)S(1)} %copy.16), channel_id=1, replica_groups=mesh['tm'=32,'chan'=16] {'chan'}, use_global_device_ids=true, to_apply=%region_3.4 | all-reduce | flops 20480 | bytes 81920 | tf_op jit(solution)/shard_map/psum | solution.py:61
  451.1 0.4 convolution_bitcast_fusion.1
  451.5 0.4 convolution_bitcast_fusion
  451.9 0.3 maximum_multiply_fusion
  452.2 1.7 copy.19
  (67 shorter events, 9.8 us)
Async XLA Ops:
  6.5 70.8 %copy-start = (bf16[128,1536]{1,0:T(8,128)(2,1)S(1)}, bf16[128,1536]{1,0:T(8,128)(2,1)}, u32[]{:S(2)}) copy-start(bf16[128,1536]{1,0:T(8,128)(2,1)} %param.4) | copy-start | bytes 1179652
  6.5 326.7 %all-reduce.3.cloned.1.call-start = ((), (), s32[]{:S(2)}) async-start(), calls=%async_computation | async-start | bytes 5242880
  91.7 0.7 copy-start.1
  91.7 2.7 copy-start.2
Sparse Core Ops, SparseCore 0:
  91.8 241.3 all-reduce.2
